TPU v7x, 128 devices: a whole 4x4x4 slice. The times are simulated.
128 devices in a mesh: rows: 16 (over y, z_lo, core), reg: 8 (over z_hi, x).
Axes of the slice: x: 4, y: 4, z: 4 (z_hi: 2, z_lo: 2; z = z_hi * 2 + z_lo), core: 2. Of those that a mesh axis runs over, the one named last changes fastest.
Arguments:
- snapshots: bfloat16 [131072, 2048], P('rows', 'reg'), may hold values from -6 to 6
- rates: bfloat16 [131072, 2048], P('rows', 'reg'), may hold values from -6 to 6
- basis: bfloat16 [131072, 128], P('rows'), may hold values from -0.015625 to 0.015625
Outputs:
- gram: float32 [8384, 8384], P('rows', 'reg')
- rhs: float32 [8384, 128], P('rows')
All inputs are finite; a program needn't handle non-finite values.
Results may differ from a plain program's by a relative error of at most 0.0042.
Values may be sent and summed in bfloat16 or wider, within the bound.
A program may use at most 64 MiB of HBM per device.

v0:
```python
import jax
import jax.numpy as jnp
import numpy as np
from jax import lax
from jax.sharding import PartitionSpec as P


def make_features(states):
    upper_i, upper_j = np.triu_indices(states.shape[0])
    quad = jnp.take(states, upper_i, axis=0) * jnp.take(states, upper_j, axis=0)
    return jnp.concatenate([states, quad], axis=0).astype(jnp.bfloat16)


def block_adder(col_feat, total, piece):
    columns = lax.slice_in_dim(col_feat, 0, piece.shape[1], axis=1)
    return total + lax.dot_general(
        piece, columns, (((1,), (1,)), ((), ())), preferred_element_type=jnp.float32
    )


def per_device(snapshots, rates, basis):
    rank = basis.shape[1]
    width = rank + rank * (rank + 1) // 2
    local_time = snapshots.shape[1]
    total_time = local_time * lax.axis_size("reg")
    row_width = width // lax.axis_size("rows")
    col_width = width // lax.axis_size("reg")
    part_states = jnp.einsum("nr,nt->rt", basis, snapshots, preferred_element_type=jnp.float32)
    part_rates = jnp.einsum("nr,nt->rt", basis, rates, preferred_element_type=jnp.float32)
    empty = jnp.zeros((row_width, col_width), jnp.float32)
    states = lax.psum_scatter(part_states, "rows", scatter_dimension=1, tiled=True)
    moments = lax.psum(part_rates, "rows")
    local_feat = make_features(states)
    row_feat = lax.all_to_all(local_feat, "rows", split_axis=0, concat_axis=1, tiled=True)
    full_feat = lax.all_gather(local_feat, "rows", axis=1, tiled=True)
    col_feat = lax.all_to_all(full_feat, "reg", split_axis=0, concat_axis=1, tiled=True)
    gram = block_adder(col_feat, empty, lax.all_gather(row_feat, "reg", axis=1, tiled=True))
    rate_half = moments.astype(jnp.bfloat16)
    rhs_part = lax.dot_general(
        row_feat, rate_half, (((1,), (1,)), ((), ())), preferred_element_type=jnp.float32
    )
    rhs = lax.psum(rhs_part, "reg")
    return (gram / float(total_time), rhs / float(total_time))


def solution(mesh):
    return jax.shard_map(
        per_device,
        mesh=mesh,
        in_specs=(P("rows", "reg"), P("rows", "reg"), P("rows", None)),
        out_specs=(P("rows", "reg"), P("rows", None)),
        check_vma=False,
    )
```

profile of v0, /device:TPU:0, one launch (start us, length us, event | category | flops | bytes accessed | tf_op | source)
XLA Modules:
  0.0 394.9 jit_solution(7418192910360525687)
XLA Ops:
  7.2 0.0 copy-start
  7.2 0.0 copy-start.2
  7.2 0.0 copy-start.3
  7.2 0.0 reduce-scatter.2.cloned.1.call-start
  7.2 1.5 copy-done
  8.8 4.6 %fusion.2 = f32[128,256]{0,1:T(8,128)} fusion(bf16[8192,128]{1,0:T(8,128)(2,1)S(1)} %copy-done, bf16[8192,256]{1,0:T(8,128)(2,1)} %param.7), kind=kOutput, calls=%fused_computation.9 | convolution fusion | flops 536870912 | bytes 6422528 | tf_op jit(solution)/shard_map/nr,nt->rt/dot_general | solution.py:28
  13.3 0.0 reduce-scatter.2.cloned.1.call-update
  13.4 0.0 all-gather.5.cloned.1.call-start
  13.4 0.0 copy-done.2
  13.4 0.0 copy-done.3
  13.5 63.4 %reduce-scatter.2.cloned.1.call-done = f32[128,16]{0,1:T(8,128)} async-done(((f32[128,256]{0,1:T(8,128)}), f32[128,16]{0,1:T(8,128)}) %reduce-scatter.2.cloned.1.call-update) | async-done | bytes 8208 | tf_op jit(solution)/shard_map/reduce_scatter | solution.py:31
  76.9 0.8 copy.22
  77.7 16.4 %gather_fusion.1 = f32[8256,16]{1,0:T(8,128)} fusion(f32[128,16]{1,0:T(8,128)S(1)} %copy.22, s32[9216]{0:T(1024)S(1)} %pad_clamp_fusion), kind=kCustom, calls=%fused_computation.1.clone | custom fusion | bytes 1089792 | tf_op jit(solution)/shard_map/jit(_take)/gather | solution.py:10
  94.1 16.3 %gather_fusion = f32[8256,16]{1,0:T(8,128)} fusion(f32[128,16]{1,0:T(8,128)S(1)} %copy.22, s32[9216]{0:T(1024)S(1)} %pad_clamp_fusion.1), kind=kCustom, calls=%fused_computation.clone | custom fusion | bytes 1089792 | tf_op jit(solution)/shard_map/jit(_take)/gather | solution.py:10
  110.4 0.0 copy-start.4
  110.4 4.8 %mul.3 = bf16[8256,16]{1,0:T(8,128)(2,1)} multiply(f32[8256,16]{1,0:T(8,128)} %gather_fusion, f32[8256,16]{1,0:T(8,128)} %gather_fusion.1) | non-fusion elementwise | flops 132096 | bytes 1320960 | tf_op jit(solution)/shard_map/mul | solution.py:10
  115.1 2.1 copy.24
  117.3 0.0 copy-done.4
  117.3 0.7 maximum_convert_fusion
  118.0 0.0 all-gather.5.cloned.1.call-update
  118.0 1.4 convert_element_type.11
  119.4 0.8 copy.25
  120.2 3.5 all-to-all-start
  123.8 0.0 all-reduce.3.cloned.1.call-start
  123.8 3.0 fusion.3
  126.8 57.9 %all-reduce.4 = bf16[128,256]{1,0:T(8,128)(2,1)S(1)} all-reduce(f32[128,256]{1,0:T(8,128)S(1)} %fusion.3), channel_id=1, replica_groups=mesh['rows'=16,'reg'=8] {'rows'}, use_global_device_ids=true, to_apply=%region_1.3 | all-reduce | flops 32768 | bytes 196608 | tf_op jit(solution)/shard_map/psum | solution.py:32
  184.7 0.0 all-to-all-done
  184.7 0.0 copy-start.1
  184.7 1.0 fusion.4
  185.7 0.0 all-reduce.3.cloned.1.call-update
  185.7 0.0 all-gather.5.cloned.1.call-done
  185.7 6.5 %copy.26 = bf16[8384,256]{1,0:T(8,128)(2,1)} copy(bf16[8384,256]{0,1:T(8,128)(2,1)} %all-gather.5.cloned.1.call-done) | data formatting | bytes 8585216 | tf_op jit(solution)/shard_map/all_gather | solution.py:35
  192.3 0.0 copy-done.1
  192.3 6.8 %all-to-all-start.1 = ((bf16[8,1048,256]{2,1,0:T(8,128)(2,1)}), bf16[8,1048,256]{2,1,0:T(8,128)(2,1)}, u32[]{:S(2)}, u32[]{:S(2)}) async-start(bf16[8,1048,256]{2,1,0:T(8,128)(2,1)} %bitcast.17), calls=%async_computation.2 | async-start | bytes 8585216 | tf_op jit(solution)/shard_map/all_to_all | solution.py:36
  199.1 0.0 all-gather.3.cloned.1.call-start
  199.1 0.5 all-gather.3.cloned.1.call-update
  199.7 119.2 %all-reduce.3.cloned.1.call-done = f32[524,128]{1,0:T(8,128)} async-done(((f32[524,128]{1,0:T(8,128)}), f32[524,128]{1,0:T(8,128)}) %all-reduce.3.cloned.1.call-update) | async-done | bytes 268304 | tf_op jit(solution)/shard_map/psum | solution.py:42
  318.9 1.7 broadcast_multiply_fusion
  320.6 0.0 all-to-all-done.1
  320.6 4.8 %copy.28 = bf16[8,131,8,256]{3,2,0,1:T(8,128)(2,1)} copy(bf16[8,131,8,256]{3,2,1,0:T(8,128)(2,1)} %bitcast.5) | data formatting | bytes 8585216 | tf_op jit(solution)/shard_map/all_to_all | solution.py:36
  325.4 54.9 %all-gather.3.cloned.1.call-done = bf16[524,2048]{0,1:T(8,128)(2,1)} async-done(((bf16[524,256]{0,1:T(8,128)(2,1)}), bf16[524,2048]{0,1:T(8,128)(2,1)}) %all-gather.3.cloned.1.call-update) | async-done | bytes 2146320 | tf_op jit(solution)/shard_map/all_gather | solution.py:37
  380.4 8.0 %convolution_multiply_fusion = f32[524,1048]{1,0:T(8,128)} fusion(bf16[524,2048]{0,1:T(8,128)(2,1)} %all-gather.3.cloned.1.call-done, bf16[1048,2048]{1,0:T(8,128)(2,1)} %bitcast.18), kind=kOutput, calls=%fused_computation.2 | convolution fusion | flops 2249875712 | bytes 8635520 | tf_op jit(solution)/shard_map/dot_general | solution.py:16
  (2 shorter events, 0.0 us)
Async XLA Ops:
  7.2 1.6 copy-start
  7.2 6.2 %copy-start.2 = (s32[8256]{0:T(1024)S(1)}, s32[8256]{0:T(1024)}, u32[]{:S(2)}) copy-start(s32[8256]{0:T(1024)} %constant.39) | copy-start | bytes 99076
  7.2 6.3 %copy-start.3 = (s32[8256]{0:T(1024)S(1)}, s32[8256]{0:T(1024)}, u32[]{:S(2)}) copy-start(s32[8256]{0:T(1024)} %constant.40) | copy-start | bytes 99076
  7.2 69.7 %reduce-scatter.2.cloned.1.call-start = ((), (), s32[]{:S(2)}) async-start(), calls=%async_computation.3 | async-start | bytes 139264 | tf_op jit(solution)/shard_map/reduce_scatter | solution.py:31
  13.4 172.4 %all-gather.5.cloned.1.call-start = ((), (), s32[]{:S(2)}) async-start(), calls=%async_computation.5 | async-start | bytes 4595712 | tf_op jit(solution)/shard_map/all_gather | solution.py:35
  110.4 6.9 %copy-start.4 = (f32[128,16]{0,1:T(8,128)S(1)}, f32[128,16]{0,1:T(8,128)}, u32[]{:S(2)}) copy-start(f32[128,16]{0,1:T(8,128)} %reduce-scatter.2.cloned.1.call-done) | copy-start | bytes 24580
  120.2 64.5 %all-to-all-start = ((bf16[16,524,16]{1,2,0:T(8,128)(2,1)}), bf16[16,524,16]{1,2,0:T(8,128)(2,1)S(1)}, u32[]{:S(2)}, u32[]{:S(2)}) async-start(bf16[16,524,16]{1,2,0:T(8,128)(2,1)} %copy.25), calls=%async_computation.1 | async-start | bytes 655360 | tf_op jit(solution)/shard_map/all_to_all | solution.py:34
  123.8 195.2 %all-reduce.3.cloned.1.call-start = ((), (), s32[]{:S(2)}) async-start(), calls=%async_computation.6 | async-start | bytes 540672 | tf_op jit(solution)/shard_map/psum | solution.py:42
  184.7 7.6 %copy-start.1 = (bf16[16,524,16]{1,2,0:T(8,128)(2,1)}, bf16[16,524,16]{1,2,0:T(8,128)(2,1)S(1)}, u32[]{:S(2)}) copy-start(bf16[16,524,16]{1,2,0:T(8,128)(2,1)S(1)} %all-to-all-done) | copy-start | bytes 804868
  192.3 128.3 %all-to-all-start.1 = ((bf16[8,1048,256]{2,1,0:T(8,128)(2,1)}), bf16[8,1048,256]{2,1,0:T(8,128)(2,1)}, u32[]{:S(2)}, u32[]{:S(2)}) async-start(bf16[8,1048,256]{2,1,0:T(8,128)(2,1)} %bitcast.17), calls=%async_computation.2 | async-start | bytes 8585216 | tf_op jit(solution)/shard_map/all_to_all | solution.py:36
  199.1 181.3 %all-gather.3.cloned.1.call-start = ((), (), s32[]{:S(2)}) async-start(), calls=%async_computation.4 | async-start | bytes 2949120 | tf_op jit(solution)/shard_map/all_gather | solution.py:37
Sparse Core Ops, SparseCore 0:
  13.5 63.3 reduce-scatter.1
  118.1 38.6 all-gather.4
  185.8 133.0 all-reduce.2
  321.7 58.6 all-gather.2
where the time goes:
time: 396 us; the launch traced here: 395 us
  waiting for transfers between devices  238 us (60%)
  blocking collectives  57.9 us (15%)
  local copies, waits for them, and re-layouts  50.7 us (13%)
  matrix products  16.6 us (4%)
  between operations  13.9 us (4%)
  starting transfers between devices  10.5 us (3%)
  other arithmetic  7.18 us (2%)
    psum x1, waiting for transfers between devices, per_device(): rhs = lax.psum(rhs_part, 'reg')  119 us
    reduce_scatter x1, waiting for transfers between devices, per_device(): lax.psum_scatter(part_states, 'rows', scatter_dimension=1, tiled=True)  63.4 us
    psum x1, blocking collectives, per_device(): moments = lax.psum(part_rates, 'rows')  57.9 us
    all_gather x1, waiting for transfers between devices, per_device(): lax.all_gather(row_feat, 'reg', axis=1, tiled=True)  54.9 us
    gather x2, local copies, waits for them, and re-layouts, make_features(): quad = jnp.take(states, upper_i, axis=0) * jnp.take(states, upper_j, axis=0)  32.7 us
    dot_general x1, matrix products, block_adder(): lax.dot_general(piece, columns, (((1,), (1,)), ((), ())), preferred_eleme...  8.05 us
  transfers between devices with their start and end apart: 6, of which 3 were waited for; matrix products, arithmetic and copies ran while one was open for 5% of the time, Pallas kernels for 0%

commit v1 on v0

--- a/solution.py
+++ b/solution.py
@@ -39,7 +39,7 @@
     rhs_part = lax.dot_general(
         row_feat, rate_half, (((1,), (1,)), ((), ())), preferred_element_type=jnp.float32
     )
-    rhs = lax.psum(rhs_part, "reg")
+    rhs = jnp.sum(lax.all_gather(rhs_part, "reg"), axis=0)
     return (gram / float(total_time), rhs / float(total_time))
 
 

time: 396 us -> 359 us (0.907)
  waiting for transfers between devices: 238 us -> 201 us
    psum x1 -> x0, waiting for transfers between devices: 119 us -> none  [per_device(): rhs = lax.psum(rhs_part, 'reg')]
    all_gather x0 -> x1, waiting for transfers between devices: none -> 83.7 us  [per_device(): rhs = jnp.sum(lax.all_gather(rhs_part, 'reg'), axis=0)]
  transfers between devices with their start and end apart: 6 -> 6, of which waited for: 3 -> 3; matrix products, arithmetic and copies ran while one was open for 5% -> 6% of each run, Pallas kernels for 0% -> 0%
where the time goes in v1:
time: 359 us; the launch traced here: 358 us
  waiting for transfers between devices  201 us (56%)
  blocking collectives  57.9 us (16%)
  local copies, waits for them, and re-layouts  50.7 us (14%)
  matrix products  16.6 us (5%)
  between operations  13.9 us (4%)
  starting transfers between devices  10.5 us (3%)
  other arithmetic  7.97 us (2%)
    all_gather x1, waiting for transfers between devices, per_device(): rhs = jnp.sum(lax.all_gather(rhs_part, 'reg'), axis=0)  83.7 us
    reduce_scatter x1, waiting for transfers between devices, per_device(): lax.psum_scatter(part_states, 'rows', scatter_dimension=1, tiled=True)  63.4 us
    psum x1, blocking collectives, per_device(): moments = lax.psum(part_rates, 'rows')  57.9 us
    all_gather x1, waiting for transfers between devices, per_device(): lax.all_gather(row_feat, 'reg', axis=1, tiled=True)  53 us
    gather x2, local copies, waits for them, and re-layouts, make_features(): quad = jnp.take(states, upper_i, axis=0) * jnp.take(states, upper_j, axis=0)  32.7 us
    dot_general x1, matrix products, block_adder(): lax.dot_general(piece, columns, (((1,), (1,)), ((), ())), preferred_eleme...  8.05 us
  transfers between devices with their start and end apart: 6, of which 3 were waited for; matrix products, arithmetic and copies ran while one was open for 6% of the time, Pallas kernels for 0%

profile of v1, /device:TPU:0, one launch (start us, length us, event | category | flops | bytes accessed | tf_op | source)
XLA Modules:
  0.0 358.2 jit_solution(16580553196007981127)
XLA Ops:
  7.2 0.0 copy-start
  7.2 0.0 copy-start.2
  7.2 0.0 copy-start.3
  7.2 0.0 reduce-scatter.2.cloned.1.call-start
  7.2 1.5 copy-done
  8.8 4.6 %fusion.1 = f32[128,256]{0,1:T(8,128)} fusion(bf16[8192,128]{1,0:T(8,128)(2,1)S(1)} %copy-done, bf16[8192,256]{1,0:T(8,128)(2,1)} %param.7), kind=kOutput, calls=%fused_computation.9 | convolution fusion | flops 536870912 | bytes 6422528 | tf_op jit(solution)/shard_map/nr,nt->rt/dot_general | solution.py:28
  13.3 0.0 reduce-scatter.2.cloned.1.call-update
  13.4 0.0 all-gather.8.cloned.1.call-start
  13.4 0.0 copy-done.2
  13.4 0.0 copy-done.3
  13.5 63.4 %reduce-scatter.2.cloned.1.call-done = f32[128,16]{0,1:T(8,128)} async-done(((f32[128,256]{0,1:T(8,128)}), f32[128,16]{0,1:T(8,128)}) %reduce-scatter.2.cloned.1.call-update) | async-done | bytes 8208 | tf_op jit(solution)/shard_map/reduce_scatter | solution.py:31
  76.9 0.8 copy.22
  77.7 16.4 %gather_fusion.1 = f32[8256,16]{1,0:T(8,128)} fusion(f32[128,16]{1,0:T(8,128)S(1)} %copy.22, s32[9216]{0:T(1024)S(1)} %pad_clamp_fusion), kind=kCustom, calls=%fused_computation.1.clone | custom fusion | bytes 1089792 | tf_op jit(solution)/shard_map/jit(_take)/gather | solution.py:10
  94.1 16.3 %gather_fusion = f32[8256,16]{1,0:T(8,128)} fusion(f32[128,16]{1,0:T(8,128)S(1)} %copy.22, s32[9216]{0:T(1024)S(1)} %pad_clamp_fusion.1), kind=kCustom, calls=%fused_computation.clone | custom fusion | bytes 1089792 | tf_op jit(solution)/shard_map/jit(_take)/gather | solution.py:10
  110.4 0.0 copy-start.4
  110.4 4.8 %mul.3 = bf16[8256,16]{1,0:T(8,128)(2,1)} multiply(f32[8256,16]{1,0:T(8,128)} %gather_fusion, f32[8256,16]{1,0:T(8,128)} %gather_fusion.1) | non-fusion elementwise | flops 132096 | bytes 1320960 | tf_op jit(solution)/shard_map/mul | solution.py:10
  115.1 2.1 copy.24
  117.3 0.0 copy-done.4
  117.3 0.7 maximum_convert_fusion
  118.0 0.0 all-gather.8.cloned.1.call-update
  118.0 1.4 convert_element_type.11
  119.4 0.8 copy.25
  120.2 3.5 all-to-all-start
  123.8 0.0 all-gather.10.cloned.1.call-start
  123.8 3.0 fusion.2
  126.8 57.9 %all-reduce.1 = bf16[128,256]{1,0:T(8,128)(2,1)S(1)} all-reduce(f32[128,256]{1,0:T(8,128)S(1)} %fusion.2), channel_id=1, replica_groups=mesh['rows'=16,'reg'=8] {'rows'}, use_global_device_ids=true, to_apply=%region_1.3 | all-reduce | flops 32768 | bytes 196608 | tf_op jit(solution)/shard_map/psum | solution.py:32
  184.7 0.0 all-to-all-done
  184.7 0.0 copy-start.1
  184.7 1.0 convolution_bitcast_fusion
  185.7 0.0 all-gather.10.cloned.1.call-update
  185.7 0.0 all-gather.8.cloned.1.call-done
  185.7 6.5 %copy.26 = bf16[8384,256]{1,0:T(8,128)(2,1)} copy(bf16[8384,256]{0,1:T(8,128)(2,1)} %all-gather.8.cloned.1.call-done) | data formatting | bytes 8585216 | tf_op jit(solution)/shard_map/all_gather | solution.py:35
  192.3 0.0 copy-done.1
  192.3 6.8 %all-to-all-start.1 = ((bf16[8,1048,256]{2,1,0:T(8,128)(2,1)}), bf16[8,1048,256]{2,1,0:T(8,128)(2,1)}, u32[]{:S(2)}, u32[]{:S(2)}) async-start(bf16[8,1048,256]{2,1,0:T(8,128)(2,1)} %bitcast.19), calls=%async_computation.2 | async-start | bytes 8585216 | tf_op jit(solution)/shard_map/all_to_all | solution.py:36
  199.1 0.0 all-gather.6.cloned.1.call-start
  199.1 0.5 all-gather.6.cloned.1.call-update
  199.7 83.7 %all-gather.10.cloned.1.call-done = f32[8,524,128]{2,1,0:T(8,128)} async-done(((f32[1,524,128]{2,1,0:T(8,128)}), f32[8,524,128]{2,1,0:T(8,128)}) %all-gather.10.cloned.1.call-update) | async-done | bytes 2146320 | tf_op jit(solution)/shard_map/all_gather | solution.py:42
  283.3 1.7 reduce_sum.9
  285.1 0.7 broadcast_multiply_fusion
  285.8 0.0 all-to-all-done.1
  285.8 4.8 %copy.28 = bf16[8,131,8,256]{3,2,0,1:T(8,128)(2,1)} copy(bf16[8,131,8,256]{3,2,1,0:T(8,128)(2,1)} %bitcast.6) | data formatting | bytes 8585216 | tf_op jit(solution)/shard_map/all_to_all | solution.py:36
  290.6 53.0 %all-gather.6.cloned.1.call-done = bf16[524,2048]{0,1:T(8,128)(2,1)} async-done(((bf16[524,256]{0,1:T(8,128)(2,1)}), bf16[524,2048]{0,1:T(8,128)(2,1)}) %all-gather.6.cloned.1.call-update) | async-done | bytes 2146320 | tf_op jit(solution)/shard_map/all_gather | solution.py:37
  343.6 8.0 %convolution_multiply_fusion = f32[524,1048]{1,0:T(8,128)} fusion(bf16[524,2048]{0,1:T(8,128)(2,1)} %all-gather.6.cloned.1.call-done, bf16[1048,2048]{1,0:T(8,128)(2,1)} %bitcast.20), kind=kOutput, calls=%fused_computation.2 | convolution fusion | flops 2249875712 | bytes 8635520 | tf_op jit(solution)/shard_map/dot_general | solution.py:16
  (2 shorter events, 0.0 us)
Async XLA Ops:
  7.2 1.6 copy-start
  7.2 6.2 %copy-start.2 = (s32[8256]{0:T(1024)S(1)}, s32[8256]{0:T(1024)}, u32[]{:S(2)}) copy-start(s32[8256]{0:T(1024)} %constant.41) | copy-start | bytes 99076
  7.2 6.3 %copy-start.3 = (s32[8256]{0:T(1024)S(1)}, s32[8256]{0:T(1024)}, u32[]{:S(2)}) copy-start(s32[8256]{0:T(1024)} %constant.42) | copy-start | bytes 99076
  7.2 69.7 %reduce-scatter.2.cloned.1.call-start = ((), (), s32[]{:S(2)}) async-start(), calls=%async_computation.3 | async-start | bytes 139264 | tf_op jit(solution)/shard_map/reduce_scatter | solution.py:31
  13.4 172.4 %all-gather.8.cloned.1.call-start = ((), (), s32[]{:S(2)}) async-start(), calls=%async_computation.5 | async-start | bytes 4595712 | tf_op jit(solution)/shard_map/all_gather | solution.py:35
  110.4 6.9 %copy-start.4 = (f32[128,16]{0,1:T(8,128)S(1)}, f32[128,16]{0,1:T(8,128)}, u32[]{:S(2)}) copy-start(f32[128,16]{0,1:T(8,128)} %reduce-scatter.2.cloned.1.call-done) | copy-start | bytes 24580
  120.2 64.5 %all-to-all-start = ((bf16[16,524,16]{1,2,0:T(8,128)(2,1)}), bf16[16,524,16]{1,2,0:T(8,128)(2,1)S(1)}, u32[]{:S(2)}, u32[]{:S(2)}) async-start(bf16[16,524,16]{1,2,0:T(8,128)(2,1)} %copy.25), calls=%async_computation.1 | async-start | bytes 655360 | tf_op jit(solution)/shard_map/all_to_all | solution.py:34
  123.8 159.6 %all-gather.10.cloned.1.call-start = ((), (), s32[]{:S(2)}) async-start(), calls=%async_computation.6 | async-start | bytes 2433024 | tf_op jit(solution)/shard_map/all_gather | solution.py:42
  184.7 7.6 %copy-start.1 = (bf16[16,524,16]{1,2,0:T(8,128)(2,1)}, bf16[16,524,16]{1,2,0:T(8,128)(2,1)S(1)}, u32[]{:S(2)}) copy-start(bf16[16,524,16]{1,2,0:T(8,128)(2,1)S(1)} %all-to-all-done) | copy-start | bytes 804868
  192.3 93.5 %all-to-all-start.1 = ((bf16[8,1048,256]{2,1,0:T(8,128)(2,1)}), bf16[8,1048,256]{2,1,0:T(8,128)(2,1)}, u32[]{:S(2)}, u32[]{:S(2)}) async-start(bf16[8,1048,256]{2,1,0:T(8,128)(2,1)} %bitcast.19), calls=%async_computation.2 | async-start | bytes 8585216 | tf_op jit(solution)/shard_map/all_to_all | solution.py:36
  199.1 144.5 %all-gather.6.cloned.1.call-start = ((), (), s32[]{:S(2)}) async-start(), calls=%async_computation.4 | async-start | bytes 2949120 | tf_op jit(solution)/shard_map/all_gather | solution.py:37
Sparse Core Ops, SparseCore 0:
  13.5 63.3 reduce-scatter.1
  118.1 38.6 all-gather.7
  185.8 97.4 all-gather.9
  286.1 57.5 all-gather.5
